TPU v7x, 256 devices: a whole 4x4x8 slice. The times are simulated.
256 devices in a mesh: seed: 4 (over x), chan: 16 (over z, y_lo), fsdp: 4 (over y_hi, core).
Axes of the slice: x: 4, y: 4 (y_hi: 2, y_lo: 2; y = y_hi * 2 + y_lo), z: 8, core: 2. Of those that a mesh axis runs over, the one named last changes fastest.
Arguments:
- stream: bfloat16 [256, 144, 8192], P(('seed', 'fsdp'), None, 'chan'), parts along dimension 0, may hold values from -12.5 to 9.5
- mid: bfloat16 [256, 144, 2048], P(('seed', 'fsdp'), None, 'chan'), parts along dimension 0, may hold values from 0 to 2
- conv_weight: bfloat16 [8192, 8192], P(('seed', 'fsdp'), 'chan'), parts along dimension 0, may hold values from -0.125 to 0.125
- head_weight: bfloat16 [32768, 16384], P(('seed', 'chan'), 'fsdp'), parts along dimension 0, may hold values from -0.375 to 0.375
- labels: int32 [64], replicated, may hold values from 0 to 16383
- proj_act: bfloat16 [2048, 32], replicated, may hold values from -0.125 to 0.125
- proj_err: bfloat16 [8192, 64], P('chan'), may hold values from -6 to 6
Outputs:
- grad_proj: float32 [256, 2048], P(('seed', 'fsdp'), 'chan'), parts along dimension 0
There are 4 independent parts, one for each index of `seed`. A program takes and returns all parts, laid end to end along the dimension named above; an argument that names none is the same for every part. Nothing has to cross between parts.
All inputs are finite; a program needn't handle non-finite values.
Results may differ from a plain program's by a relative error of at most 0.01.
Values may be sent and summed in bfloat16 or wider, within the bound.
No kernel may reach another device: no remote copies, remote signals or barrier semaphores. Data moves between devices by JAX's collectives and lax.ppermute only.
A program may use at most 64 MiB of HBM per device.

v0:
```python
import jax
import jax.numpy as jnp
from jax import lax
from jax.sharding import PartitionSpec as P


def per_device(stream, mid, conv_weight, head_weight, labels, proj_act, proj_err):
    images = stream.shape[0]
    positions = stream.shape[1]
    width = stream.shape[2]
    rows = images * positions
    gathered = lax.all_gather(mid, "chan", axis=2, tiled=True)
    mid_rows = gathered.reshape(rows, gathered.shape[2])
    conv_out = jnp.dot(
        mid_rows,
        lax.all_gather(conv_weight, "fsdp", axis=0, tiled=True),
        preferred_element_type=jnp.float32,
    )
    acts_proj = jnp.dot(mid_rows, proj_act, preferred_element_type=jnp.float32)
    y_local = stream.astype(jnp.float32) + conv_out.reshape(images, positions, width)
    pooled = jnp.mean(jnp.maximum(y_local, 0.0), axis=1).astype(jnp.bfloat16)
    pooled_all = lax.all_gather(pooled, "fsdp", axis=0, tiled=True)
    partial_value = jnp.dot(pooled_all, head_weight, preferred_element_type=jnp.float32)
    block = head_weight.shape[1]
    block_start = lax.axis_index("fsdp") * block
    logits = lax.psum(partial_value, "chan")
    expo = jnp.exp(logits)
    total = lax.psum(jnp.sum(expo, axis=1), "fsdp")
    classes = block_start + jnp.arange(block, dtype=jnp.int32)
    onehot = (labels[:, None] == classes[None, :]).astype(jnp.float32)
    dlogits = (expo / total[:, None] - onehot).astype(jnp.bfloat16)
    dpooled = lax.psum_scatter(
        lax.dot_general(
            dlogits, head_weight, (((1,), (1,)), ((), ())), preferred_element_type=jnp.float32
        ),
        "fsdp",
        scatter_dimension=0,
        tiled=True,
    )
    error = jnp.where(y_local > 0.0, dpooled[:, None, :] / positions, 0.0).astype(jnp.bfloat16)
    err_part = jnp.dot(error.reshape(rows, width), proj_err, preferred_element_type=jnp.float32)
    acts_cube = acts_proj.reshape(images, positions, acts_proj.shape[1])
    err_full = lax.psum(err_part.astype(jnp.bfloat16), "chan").astype(jnp.float32)
    grads = jnp.einsum(
        "npa,npb->nab",
        acts_cube,
        err_full.reshape(images, positions, err_full.shape[1]),
        precision=lax.Precision.HIGHEST,
    )
    grads = grads.reshape(images, -1)
    share = grads.shape[1] // lax.axis_size("chan")
    return lax.dynamic_slice_in_dim(grads, lax.axis_index("chan") * share, share, 1)


def solution(mesh):
    in_specs = (
        P(("seed", "fsdp"), None, "chan"),
        P(("seed", "fsdp"), None, "chan"),
        P(("seed", "fsdp"), "chan"),
        P(("seed", "chan"), "fsdp"),
        P(),
        P(),
        P("chan", None),
    )
    out_specs = P(("seed", "fsdp"), "chan")
    return jax.shard_map(
        per_device, mesh=mesh, in_specs=in_specs, out_specs=out_specs, check_vma=False
    )
```

profile of v0, /device:TPU:2, one launch (start us, length us, event | category | flops | bytes accessed | tf_op | source)
XLA Modules:
  0.0 618.6 jit_solution(5644417789808126572)
XLA Ops:
  6.5 0.0 copy-start
  6.5 0.7 all-gather.5.cloned.1.call-update
  7.3 0.0 all-gather.3.cloned.1.call-start
  7.3 0.7 all-gather.3.cloned.1.call-update
  8.0 0.0 all-reduce.3.cloned.1.call-start
  8.1 33.3 %all-gather.5.cloned.1.call-done = bf16[2048,512]{1,0:T(8,128)(2,1)} async-done(((bf16[512,512]{1,0:T(8,128)(2,1)}), bf16[2048,512]{1,0:T(8,128)(2,1)}) %all-gather.5.cloned.1.call-update) | async-done | bytes 2097168 | tf_op jit(solution)/shard_map/all_gather | solution.py:16
  41.4 217.4 %all-gather.3.cloned.1.call-done = bf16[16,144,2048]{2,1,0:T(8,128)(2,1)} async-done(((bf16[16,144,128]{2,1,0:T(8,128)(2,1)}), bf16[16,144,2048]{2,1,0:T(8,128)(2,1)}) %all-gather.3.cloned.1.call-update) | async-done | bytes 9437200 | tf_op jit(solution)/shard_map/all_gather | solution.py:12
  258.7 11.5 %maximum_reduce_fusion = (f32[16,512]{1,0:T(8,128)S(1)}, f32[16,144,512]{2,1,0:T(8,128)}) fusion(bf16[16,144,512]{2,1,0:T(8,128)(2,1)} %param.7, bf16[16,144,2048]{2,1,0:T(8,128)(2,1)} %all-gather.3.cloned.1.call-done, bf16[2048,512]{1,0:T(8,128)(2,1)} %all-gather.5.cloned.1.call-done), kind=kOutput, calls=%fused_computation.1 | convolution fusion | flops 4836548608 | bytes 18644992 | tf_op jit(solution)/shard_map/dot_general | solution.py:14
  270.3 6.8 %all_gather.11 = bf16[64,512]{1,0:T(8,128)(2,1)S(1)} all-gather(bf16[16,512]{1,0:T(8,128)(2,1)S(1)} %multiply_convert_fusion), channel_id=1, replica_groups=mesh['seed'=4,'chan'=16,'fsdp'=4] {'fsdp'}, dimensions={0}, use_global_device_ids=true | all-gather | bytes 81920 | tf_op jit(solution)/shard_map/all_gather | solution.py:22
  277.0 1.8 fusion.8
  278.9 0.0 all-reduce.3.cloned.1.call-update
  278.9 0.0 reduce-scatter.2.cloned.1.call-start
  279.0 0.0 copy-start.2
  279.0 142.3 %all-reduce.3.cloned.1.call-done = f32[64,4096]{1,0:T(8,128)} async-done(((f32[64,4096]{1,0:T(8,128)}), f32[64,4096]{1,0:T(8,128)}) %all-reduce.3.cloned.1.call-update) | async-done | bytes 1048592 | tf_op jit(solution)/shard_map/psum | solution.py:26
  421.2 1.5 exponential_reduce_fusion
  422.7 7.2 %psum.22 = f32[64]{0:T(128)S(1)} all-reduce(f32[64]{0:T(128)S(1)} %exponential_reduce_fusion), channel_id=1, replica_groups=mesh['seed'=4,'chan'=16,'fsdp'=4] {'fsdp'}, use_global_device_ids=true, to_apply=%region_3.0 | all-reduce | flops 64 | bytes 512 | tf_op jit(solution)/shard_map/psum | solution.py:28
  429.9 4.6 fusion.2
  434.5 0.0 reduce-scatter.2.cloned.1.call-update
  434.5 0.0 all-reduce.5.cloned.1.call-start
  434.6 31.8 %reduce-scatter.2.cloned.1.call-done = f32[16,512]{1,0:T(8,128)} async-done(((f32[64,512]{1,0:T(8,128)}), f32[16,512]{1,0:T(8,128)}) %reduce-scatter.2.cloned.1.call-update) | async-done | bytes 32784 | tf_op jit(solution)/shard_map/reduce_scatter | solution.py:32
  466.4 0.8 broadcast_multiply_fusion
  467.2 0.0 copy-done.2
  467.2 3.2 select_convert_fusion
  470.4 0.8 convolution_convert_fusion
  471.2 0.9 reshape.25
  472.1 0.9 copy.8
  473.0 0.0 all-reduce.5.cloned.1.call-update
  473.1 6.9 %fusion.6 = f32[16,144,32]{1,2,0:T(8,128)S(1)} fusion(bf16[16,144,2048]{2,1,0:T(8,128)(2,1)} %all-gather.3.cloned.1.call-done, bf16[2048,32]{0,1:T(8,128)(2,1)S(1)} %copy-done), kind=kOutput, calls=%fused_computation.12 | convolution fusion | flops 301989888 | bytes 9863168 | tf_op jit(solution)/shard_map/dot_general | solution.py:19
  480.0 129.8 %all-reduce.5.cloned.1.call-done = bf16[16,144,64]{1,2,0:T(8,128)(2,1)} async-done(((bf16[16,144,64]{1,2,0:T(8,128)(2,1)}), bf16[16,144,64]{1,2,0:T(8,128)(2,1)}) %all-reduce.5.cloned.1.call-update) | async-done | bytes 294928 | tf_op jit(solution)/shard_map/psum | solution.py:43
  609.7 1.6 fusion.9
  611.3 0.1 reshape.26
  611.4 0.6 constant_dynamic-slice_fusion
  (10 shorter events, 0.0 us)
Async XLA Ops:
  6.5 466.5 %copy-start = (bf16[2048,32]{0,1:T(8,128)(2,1)S(1)}, bf16[2048,32]{0,1:T(8,128)(2,1)}, u32[]{:S(2)}) copy-start(bf16[2048,32]{0,1:T(8,128)(2,1)} %param.12) | copy-start | bytes 393220
  6.5 34.8 %all-gather.5.cloned.1.call-start = ((), (), s32[]{:S(2)}) async-start(), calls=%async_computation.2 | async-start | bytes 2621440 | tf_op jit(solution)/shard_map/all_gather | solution.py:16
  7.3 251.5 %all-gather.3.cloned.1.call-start = ((), (), s32[]{:S(2)}) async-start(), calls=%async_computation.1 | async-start | bytes 10027008 | tf_op jit(solution)/shard_map/all_gather | solution.py:12
  8.0 413.2 %all-reduce.3.cloned.1.call-start = ((), (), s32[]{:S(2)}) async-start(), calls=%async_computation.3 | async-start | bytes 2097152 | tf_op jit(solution)/shard_map/psum | solution.py:26
  258.7 18.3 %copy-start.1 = (bf16[512,4096]{1,0:T(8,128)(2,1)S(1)}, bf16[512,4096]{1,0:T(8,128)(2,1)}, u32[]{:S(2)}) copy-start(bf16[512,4096]{1,0:T(8,128)(2,1)} %param.10) | copy-start | bytes 12582916
  270.3 159.6 %copy-start.4 = (s32[64]{0:T(128)S(1)}, s32[64]{0:T(128)}, u32[]{:S(2)}) copy-start(s32[64]{0:T(128)} %param.11) | copy-start | bytes 772
  278.9 187.5 %reduce-scatter.2.cloned.1.call-start = ((), (), s32[]{:S(2)}) async-start(), calls=%async_computation.4 | async-start | bytes 163840 | tf_op jit(solution)/shard_map/reduce_scatter | solution.py:32
  279.0 188.2 %copy-start.2 = (bf16[16,144,512]{2,1,0:T(8,128)(2,1)S(1)}, bf16[16,144,512]{2,1,0:T(8,128)(2,1)}, u32[]{:S(2)}) copy-start(bf16[16,144,512]{2,1,0:T(8,128)(2,1)} %param.7) | copy-start | bytes 7077892
  434.5 175.2 %all-reduce.5.cloned.1.call-start = ((), (), s32[]{:S(2)}) async-start(), calls=%async_computation.5 | async-start | bytes 1048576 | tf_op jit(solution)/shard_map/psum | solution.py:43
  467.2 3.2 copy-start.3
Sparse Core Ops, SparseCore 0:
  9.2 32.1 all-gather.4
  43.1 215.6 all-gather.2
  279.0 142.1 all-reduce.2
  434.6 31.7 reduce-scatter.1
  473.2 136.5 all-reduce.4
where the time goes:
time: 619 us
  waiting for transfers between devices  556 us (90%)
  matrix products  27.2 us (4%)
  blocking collectives  13.9 us (2%)
  between operations  13.2 us (2%)
    all_gather x1, waiting for transfers between devices, per_device(): gathered = lax.all_gather(mid, 'chan', axis=2, tiled=True)  217 us
    psum x1, waiting for transfers between devices, per_device(): logits = lax.psum(partial_value, 'chan')  142 us
    psum x1, waiting for transfers between devices, per_device(): lax.psum(err_part.astype(jnp.bfloat16), 'chan').astype(jnp.float32)  130 us
    all_gather x1, waiting for transfers between devices, per_device(): lax.all_gather(conv_weight, 'fsdp', axis=0, tiled=True)  33.3 us
    reduce_scatter x1, waiting for transfers between devices, per_device(): lax.psum_scatter(lax.dot_general(dlogits, head_weight, (((1,), (1,)), (()...  31.8 us
  transfers between devices with their start and end apart: 5, of which 5 were waited for; matrix products, arithmetic and copies ran while one was open for 1% of the time, Pallas kernels for 0%

commit v1 on v0

--- a/solution.py
+++ b/solution.py
@@ -23,7 +23,7 @@
     partial_value = jnp.dot(pooled_all, head_weight, preferred_element_type=jnp.float32)
     block = head_weight.shape[1]
     block_start = lax.axis_index("fsdp") * block
-    logits = lax.psum(partial_value, "chan")
+    logits = jnp.sum(lax.all_gather(partial_value, "chan"), axis=0)
     expo = jnp.exp(logits)
     total = lax.psum(jnp.sum(expo, axis=1), "fsdp")
     classes = block_start + jnp.arange(block, dtype=jnp.int32)

time: 619 us -> 843 us (1.36)
  waiting for transfers between devices: 556 us -> 771 us
    all_gather x0 -> x1, waiting for transfers between devices: none -> 354 us  [per_device(): logits = jnp.sum(lax.all_gather(partial_value, 'chan'), axis=0)]
    psum x1 -> x0, waiting for transfers between devices: 142 us -> none  [per_device(): logits = lax.psum(partial_value, 'chan')]
where the time goes in v1:
time: 843 us; the launch traced here: 842 us
  waiting for transfers between devices  771 us (91%)
  matrix products  26.9 us (3%)
  blocking collectives  17 us (2%)
  between operations  13.2 us (2%)
  other arithmetic  11.6 us (1%)
    all_gather x1, waiting for transfers between devices, per_device(): logits = jnp.sum(lax.all_gather(partial_value, 'chan'), axis=0)  354 us
    all_gather x1, waiting for transfers between devices, per_device(): gathered = lax.all_gather(mid, 'chan', axis=2, tiled=True)  217 us
    psum x1, waiting for transfers between devices, per_device(): lax.psum(err_part.astype(jnp.bfloat16), 'chan').astype(jnp.float32)  130 us
    reduce_scatter x1, waiting for transfers between devices, per_device(): lax.psum_scatter(lax.dot_general(dlogits, head_weight, (((1,), (1,)), (()...  34.8 us
    all_gather x1, waiting for transfers between devices, per_device(): lax.all_gather(conv_weight, 'fsdp', axis=0, tiled=True)  33.3 us
  transfers between devices with their start and end apart: 5, of which 5 were waited for; matrix products, arithmetic and copies ran while one was open for 1% of the time, Pallas kernels for 0%

profile of v1, /device:TPU:2, one launch (start us, length us, event | category | flops | bytes accessed | tf_op | source)
XLA Modules:
  0.0 842.2 jit_solution(2939977555672321725)
XLA Ops:
  6.5 0.7 all-gather.7.cloned.1.call-update
  7.3 0.0 all-gather.5.cloned.1.call-start
  7.3 0.7 all-gather.5.cloned.1.call-update
  8.0 0.0 all-gather.9.cloned.1.call-start
  8.1 33.3 %all-gather.7.cloned.1.call-done = bf16[2048,512]{1,0:T(8,128)(2,1)} async-done(((bf16[512,512]{1,0:T(8,128)(2,1)}), bf16[2048,512]{1,0:T(8,128)(2,1)}) %all-gather.7.cloned.1.call-update) | async-done | bytes 2097168 | tf_op jit(solution)/shard_map/all_gather | solution.py:16
  41.4 217.4 %all-gather.5.cloned.1.call-done = bf16[16,144,2048]{2,1,0:T(8,128)(2,1)} async-done(((bf16[16,144,128]{2,1,0:T(8,128)(2,1)}), bf16[16,144,2048]{2,1,0:T(8,128)(2,1)}) %all-gather.5.cloned.1.call-update) | async-done | bytes 9437200 | tf_op jit(solution)/shard_map/all_gather | solution.py:12
  258.7 11.6 %maximum_reduce_fusion = (f32[16,512]{1,0:T(8,128)S(1)}, f32[16,144,512]{2,1,0:T(8,128)}) fusion(bf16[16,144,512]{2,1,0:T(8,128)(2,1)} %param.7, bf16[16,144,2048]{2,1,0:T(8,128)(2,1)} %all-gather.5.cloned.1.call-done, bf16[2048,512]{1,0:T(8,128)(2,1)} %all-gather.7.cloned.1.call-done), kind=kOutput, calls=%fused_computation.1 | convolution fusion | flops 4836548608 | bytes 18644992 | tf_op jit(solution)/shard_map/dot_general | solution.py:14
  270.3 6.8 all_gather.17
  277.1 0.0 copy-done.1
  277.1 1.8 fusion.8
  278.9 0.0 all-gather.9.cloned.1.call-update
  278.9 0.0 reduce-scatter.2.cloned.1.call-start
  279.0 354.1 %all-gather.9.cloned.1.call-done = f32[1024,4096]{1,0:T(8,128)} async-done(((f32[64,4096]{1,0:T(8,128)}), f32[1024,4096]{1,0:T(8,128)}) %all-gather.9.cloned.1.call-update) | async-done | bytes 16777232 | tf_op jit(solution)/shard_map/all_gather | solution.py:26
  633.1 6.9 reduce_sum.28
  640.0 0.0 copy-start.2
  640.0 0.8 exponential_reduce_fusion
  640.7 10.2 %psum.14 = f32[64]{0:T(128)} all-reduce(f32[64]{0:T(128)} %exponential_reduce_fusion), channel_id=1, replica_groups=mesh['seed'=4,'chan'=16,'fsdp'=4] {'fsdp'}, use_global_device_ids=true, to_apply=%region_3.0 | all-reduce | flops 64 | bytes 512 | tf_op jit(solution)/shard_map/psum | solution.py:28
  651.0 4.3 fusion.2
  655.3 0.0 reduce-scatter.2.cloned.1.call-update
  655.3 0.0 all-reduce.2.cloned.1.call-start
  655.3 34.8 %reduce-scatter.2.cloned.1.call-done = f32[16,512]{1,0:T(8,128)} async-done(((f32[64,512]{1,0:T(8,128)}), f32[16,512]{1,0:T(8,128)}) %reduce-scatter.2.cloned.1.call-update) | async-done | bytes 32784 | tf_op jit(solution)/shard_map/reduce_scatter | solution.py:32
  690.1 0.8 broadcast_multiply_fusion
  690.9 3.2 select_convert_fusion
  694.1 0.8 convolution_convert_fusion
  694.9 0.9 reshape.25
  695.8 1.0 copy.9
  696.7 0.0 all-reduce.2.cloned.1.call-update
  696.8 6.9 fusion.6
  703.7 129.7 %all-reduce.2.cloned.1.call-done = bf16[16,144,64]{1,2,0:T(8,128)(2,1)} async-done(((bf16[16,144,64]{1,2,0:T(8,128)(2,1)}), bf16[16,144,64]{1,2,0:T(8,128)(2,1)}) %all-reduce.2.cloned.1.call-update) | async-done | bytes 294928 | tf_op jit(solution)/shard_map/psum | solution.py:43
  833.4 1.6 fusion.9
  835.0 0.1 reshape.26
  835.1 0.6 constant_dynamic-slice_fusion
  (9 shorter events, 0.0 us)
Async XLA Ops:
  6.5 690.2 %copy-start = (bf16[2048,32]{0,1:T(8,128)(2,1)S(1)}, bf16[2048,32]{0,1:T(8,128)(2,1)}, u32[]{:S(2)}) copy-start(bf16[2048,32]{0,1:T(8,128)(2,1)} %param.12) | copy-start | bytes 393220
  6.5 34.8 %all-gather.7.cloned.1.call-start = ((), (), s32[]{:S(2)}) async-start(), calls=%async_computation.2 | async-start | bytes 2621440 | tf_op jit(solution)/shard_map/all_gather | solution.py:16
  7.3 251.5 %all-gather.5.cloned.1.call-start = ((), (), s32[]{:S(2)}) async-start(), calls=%async_computation.1 | async-start | bytes 10027008 | tf_op jit(solution)/shard_map/all_gather | solution.py:12
  8.0 625.1 %all-gather.9.cloned.1.call-start = ((), (), s32[]{:S(2)}) async-start(), calls=%async_computation.5 | async-start | bytes 17825792 | tf_op jit(solution)/shard_map/all_gather | solution.py:26
  258.7 18.3 %copy-start.1 = (bf16[512,4096]{1,0:T(8,128)(2,1)S(1)}, bf16[512,4096]{1,0:T(8,128)(2,1)}, u32[]{:S(2)}) copy-start(bf16[512,4096]{1,0:T(8,128)(2,1)} %param.10) | copy-start | bytes 12582916
  278.9 411.2 %reduce-scatter.2.cloned.1.call-start = ((), (), s32[]{:S(2)}) async-start(), calls=%async_computation.3 | async-start | bytes 163840 | tf_op jit(solution)/shard_map/reduce_scatter | solution.py:32
  640.0 50.9 %copy-start.2 = (bf16[16,144,512]{2,1,0:T(8,128)(2,1)S(1)}, bf16[16,144,512]{2,1,0:T(8,128)(2,1)}, u32[]{:S(2)}) copy-start(bf16[16,144,512]{2,1,0:T(8,128)(2,1)} %param.7) | copy-start | bytes 7077892
  655.3 178.1 %all-reduce.2.cloned.1.call-start = ((), (), s32[]{:S(2)}) async-start(), calls=%async_computation.4 | async-start | bytes 1048576 | tf_op jit(solution)/shard_map/psum | solution.py:43
  690.9 3.2 copy-start.3
Sparse Core Ops, SparseCore 0:
  9.2 32.1 all-gather.6
  43.1 215.6 all-gather.4
  279.0 354.0 all-gather.8
  655.4 34.6 reduce-scatter.1
  696.9 136.4 all-reduce.1

commit v2 on v0

--- a/solution.py
+++ b/solution.py
@@ -13,7 +13,9 @@
     mid_rows = gathered.reshape(rows, gathered.shape[2])
     conv_out = jnp.dot(
         mid_rows,
-        lax.all_gather(conv_weight, "fsdp", axis=0, tiled=True),
+        jnp.concatenate(
+            lax.all_to_all(jnp.stack([conv_weight] * lax.axis_size("fsdp")), "fsdp", 0, 0), axis=0
+        ),
         preferred_element_type=jnp.float32,
     )
     acts_proj = jnp.dot(mid_rows, proj_act, preferred_element_type=jnp.float32)

time: 619 us -> 599 us (0.968)
  waiting for transfers between devices: 556 us -> 477 us
  blocking collectives: 13.9 us -> 71.8 us
    all_to_all x0 -> x1, blocking collectives: none -> 57.9 us  [per_device(): lax.all_to_all(jnp.stack([conv_weight] * lax.axis_size('fsdp')), 'fsdp',...]
    all_gather x1, waiting for transfers between devices: 217 us -> 169 us  [per_device(): gathered = lax.all_gather(mid, 'chan', axis=2, tiled=True)]
    all_gather x1 -> x0, waiting for transfers between devices: 33.3 us -> none  [per_device(): lax.all_gather(conv_weight, 'fsdp', axis=0, tiled=True)]
  transfers between devices with their start and end apart: 5 -> 4, of which waited for: 5 -> 4; matrix products, arithmetic and copies ran while one was open for 1% -> 1% of each run, Pallas kernels for 0% -> 0%
where the time goes in v2:
time: 599 us; the launch traced here: 598 us
  waiting for transfers between devices  477 us (80%)
  blocking collectives  71.8 us (12%)
  matrix products  26.9 us (4%)
  between operations  13.2 us (2%)
    all_gather x1, waiting for transfers between devices, per_device(): gathered = lax.all_gather(mid, 'chan', axis=2, tiled=True)  169 us
    psum x1, waiting for transfers between devices, per_device(): logits = lax.psum(partial_value, 'chan')  146 us
    psum x1, waiting for transfers between devices, per_device(): lax.psum(err_part.astype(jnp.bfloat16), 'chan').astype(jnp.float32)  130 us
    all_to_all x1, blocking collectives, per_device(): lax.all_to_all(jnp.stack([conv_weight] * lax.axis_size('fsdp')), 'fsdp',...  57.9 us
    reduce_scatter x1, waiting for transfers between devices, per_device(): lax.psum_scatter(lax.dot_general(dlogits, head_weight, (((1,), (1,)), (()...  31.8 us
  transfers between devices with their start and end apart: 4, of which 4 were waited for; matrix products, arithmetic and copies ran while one was open for 1% of the time, Pallas kernels for 0%

profile of v2, /device:TPU:2, one launch (start us, length us, event | category | flops | bytes accessed | tf_op | source)
XLA Modules:
  0.0 598.3 jit_solution(13380078710502289216)
XLA Ops:
  6.5 0.0 copy-start
  6.5 0.0 all-gather.2.cloned.1.call-start
  6.5 0.7 all-gather.2.cloned.1.call-update
  7.3 0.0 all-reduce.3.cloned.1.call-start
  7.3 1.2 stack.2
  8.5 57.9 %all_to_all.5 = bf16[4,512,512]{2,1,0:T(8,128)(2,1)} all-to-all(bf16[4,512,512]{2,1,0:T(8,128)(2,1)S(1)} %stack.2), channel_id=1, replica_groups=mesh['seed'=4,'chan'=16,'fsdp'=4] {'fsdp'}, dimensions={0} | all-to-all | bytes 4194304 | tf_op jit(solution)/shard_map/all_to_all | solution.py:17
  66.4 169.1 %all-gather.2.cloned.1.call-done = bf16[16,144,2048]{2,1,0:T(8,128)(2,1)} async-done(((bf16[16,144,128]{2,1,0:T(8,128)(2,1)}), bf16[16,144,2048]{2,1,0:T(8,128)(2,1)}) %all-gather.2.cloned.1.call-update) | async-done | bytes 9437200 | tf_op jit(solution)/shard_map/all_gather | solution.py:12
  235.5 0.0 copy-done.2
  235.5 11.2 %maximum_reduce_fusion = (f32[16,512]{1,0:T(8,128)S(1)}, f32[16,144,512]{2,1,0:T(8,128)}) fusion(bf16[16,144,512]{2,1,0:T(8,128)(2,1)S(1)} %copy-done.2, bf16[16,144,2048]{2,1,0:T(8,128)(2,1)} %all-gather.2.cloned.1.call-done, bf16[2048,512,1]{1,0,2:T(8,128)(2,1)} %bitcast.20), kind=kOutput, calls=%fused_computation.1 | convolution fusion | flops 4836548608 | bytes 18644992 | tf_op jit(solution)/shard_map/dot_general | solution.py:14
  246.8 6.8 %all_gather.7 = bf16[64,512]{1,0:T(8,128)(2,1)S(1)} all-gather(bf16[16,512]{1,0:T(8,128)(2,1)S(1)} %multiply_convert_fusion), channel_id=1, replica_groups=mesh['seed'=4,'chan'=16,'fsdp'=4] {'fsdp'}, dimensions={0}, use_global_device_ids=true | all-gather | bytes 81920 | tf_op jit(solution)/shard_map/all_gather | solution.py:24
  253.5 0.0 copy-done.1
  253.5 1.9 fusion.6
  255.4 0.0 all-reduce.3.cloned.1.call-update
  255.4 0.0 reduce-scatter.2.cloned.1.call-start
  255.5 145.6 %all-reduce.3.cloned.1.call-done = f32[64,4096]{1,0:T(8,128)} async-done(((f32[64,4096]{1,0:T(8,128)}), f32[64,4096]{1,0:T(8,128)}) %all-reduce.3.cloned.1.call-update) | async-done | bytes 1048592 | tf_op jit(solution)/shard_map/psum | solution.py:28
  401.0 1.5 exponential_reduce_fusion
  402.5 7.2 %psum.22 = f32[64]{0:T(128)S(1)} all-reduce(f32[64]{0:T(128)S(1)} %exponential_reduce_fusion), channel_id=1, replica_groups=mesh['seed'=4,'chan'=16,'fsdp'=4] {'fsdp'}, use_global_device_ids=true, to_apply=%region_3.0 | all-reduce | flops 64 | bytes 512 | tf_op jit(solution)/shard_map/psum | solution.py:30
  409.7 4.6 fusion
  414.3 0.0 reduce-scatter.2.cloned.1.call-update
  414.3 0.0 all-reduce.5.cloned.1.call-start
  414.3 31.8 %reduce-scatter.2.cloned.1.call-done = f32[16,512]{1,0:T(8,128)} async-done(((f32[64,512]{1,0:T(8,128)}), f32[16,512]{1,0:T(8,128)}) %reduce-scatter.2.cloned.1.call-update) | async-done | bytes 32784 | tf_op jit(solution)/shard_map/reduce_scatter | solution.py:34
  446.2 0.8 broadcast_multiply_fusion
  446.9 3.2 select_convert_fusion
  450.2 0.8 convolution_convert_fusion
  451.0 0.9 reshape.31
  451.9 0.9 copy.8
  452.8 0.0 all-reduce.5.cloned.1.call-update
  452.8 6.9 %fusion.4 = f32[16,144,32]{1,2,0:T(8,128)S(1)} fusion(bf16[16,144,2048]{2,1,0:T(8,128)(2,1)} %all-gather.2.cloned.1.call-done, bf16[2048,32]{0,1:T(8,128)(2,1)S(1)} %copy-done), kind=kOutput, calls=%fused_computation.10 | convolution fusion | flops 301989888 | bytes 9863168 | tf_op jit(solution)/shard_map/dot_general | solution.py:21
  459.7 129.8 %all-reduce.5.cloned.1.call-done = bf16[16,144,64]{1,2,0:T(8,128)(2,1)} async-done(((bf16[16,144,64]{1,2,0:T(8,128)(2,1)}), bf16[16,144,64]{1,2,0:T(8,128)(2,1)}) %all-reduce.5.cloned.1.call-update) | async-done | bytes 294928 | tf_op jit(solution)/shard_map/psum | solution.py:45
  589.5 1.6 fusion.7
  591.1 0.1 reshape.32
  591.2 0.6 constant_dynamic-slice_fusion
  (9 shorter events, 0.0 us)
Async XLA Ops:
  6.5 446.3 %copy-start = (bf16[2048,32]{0,1:T(8,128)(2,1)S(1)}, bf16[2048,32]{0,1:T(8,128)(2,1)}, u32[]{:S(2)}) copy-start(bf16[2048,32]{0,1:T(8,128)(2,1)} %param.12) | copy-start | bytes 393220
  6.5 229.0 %copy-start.2 = (bf16[16,144,512]{2,1,0:T(8,128)(2,1)S(1)}, bf16[16,144,512]{2,1,0:T(8,128)(2,1)}, u32[]{:S(2)}) copy-start(bf16[16,144,512]{2,1,0:T(8,128)(2,1)} %param.7) | copy-start | bytes 7077892
  6.5 229.0 %all-gather.2.cloned.1.call-start = ((), (), s32[]{:S(2)}) async-start(), calls=%async_computation.2 | async-start | bytes 10027008 | tf_op jit(solution)/shard_map/all_gather | solution.py:12
  7.3 393.8 %all-reduce.3.cloned.1.call-start = ((), (), s32[]{:S(2)}) async-start(), calls=%async_computation.3 | async-start | bytes 2097152 | tf_op jit(solution)/shard_map/psum | solution.py:28
  235.5 18.0 %copy-start.1 = (bf16[512,4096]{1,0:T(8,128)(2,1)S(1)}, bf16[512,4096]{1,0:T(8,128)(2,1)}, u32[]{:S(2)}) copy-start(bf16[512,4096]{1,0:T(8,128)(2,1)} %param.10) | copy-start | bytes 12582916
  246.8 162.9 %copy-start.4 = (s32[64]{0:T(128)S(1)}, s32[64]{0:T(128)}, u32[]{:S(2)}) copy-start(s32[64]{0:T(128)} %param.11) | copy-start | bytes 772
  255.4 190.8 %reduce-scatter.2.cloned.1.call-start = ((), (), s32[]{:S(2)}) async-start(), calls=%async_computation.4 | async-start | bytes 163840 | tf_op jit(solution)/shard_map/reduce_scatter | solution.py:34
  414.3 175.2 %all-reduce.5.cloned.1.call-start = ((), (), s32[]{:S(2)}) async-start(), calls=%async_computation.5 | async-start | bytes 1048576 | tf_op jit(solution)/shard_map/psum | solution.py:45
  446.9 3.2 copy-start.3
Sparse Core Ops, SparseCore 0:
  9.1 226.4 all-gather.1
  255.5 145.4 all-reduce.2
  414.4 31.7 reduce-scatter.1
  452.9 136.4 all-reduce.4
